TPU v7x, 256 devices: a whole 4x4x8 slice. The times are simulated.
256 devices in a mesh: row: 32 (over x_hi, z, core), col: 8 (over y, x_lo).
Axes of the slice: x: 4 (x_hi: 2, x_lo: 2; x = x_hi * 2 + x_lo), y: 4, z: 8, core: 2. Of those that a mesh axis runs over, the one named last changes fastest.
Arguments:
- p_tiles: bfloat16 [1024, 2, 128, 128], P(('row', 'col')), may hold values from -0.5 to 0.5
- p_cols: int32 [1024, 2], P(('row', 'col')), may hold values from 0 to 31, as said below
- q_tiles: bfloat16 [1024, 6, 128, 128], P(('row', 'col')), may hold values from -1.796875 to 1.796875
- q_cols: int32 [1024, 6], P(('row', 'col')), may hold values from 0 to 31, all different within a row
Outputs:
- coarse: float32 [4096, 4096], P('row', 'col')
Inputs may be any that keep to these rules, and one draw needn't show every extreme that they name: `p_cols`: the 2 coarse tiles in one row differ; among the fine blocks held by the devices of one index of col, every coarse tile is named at least once and at most 16 times, and some tile exactly 16 times. `q_cols`: the 6 coarse tiles in one row differ; every coarse tile appears somewhere.
All inputs are finite; a program needn't handle non-finite values.
Results may differ from a plain program's by a relative error of at most 0.0003.
Values may be sent and summed in bfloat16 or wider, within the bound.
A program may use at most 128 MiB of HBM per device.

v0:
```python
import math
import jax
import jax.numpy as jnp
from jax import lax
from jax.sharding import PartitionSpec as P


def spread_tiles(tile_set, columns, tile_count):
    blocks, per_block, extent, _ = tile_set.shape
    flipped = jnp.swapaxes(tile_set, 2, 3)
    fine_ids = jnp.broadcast_to(jnp.arange(blocks, dtype=jnp.int32)[:, None], (blocks, per_block))
    placed = jnp.zeros((tile_count, extent, blocks, extent), tile_set.dtype)
    placed = placed.at[columns, :, fine_ids, :].set(flipped)
    return placed.reshape(tile_count * extent, blocks * extent)


def fold_tiles(summed, transposed, tile_set, columns):
    blocks, per_block, extent, _ = tile_set.shape
    height = transposed.shape[0]
    bundle = math.gcd(blocks, 8)
    tile_groups = tile_set.reshape(blocks // bundle, bundle, per_block, extent, extent)
    column_groups = columns.reshape(blocks // bundle, bundle * per_block)

    def one_group(running, inputs):
        position, bundle_tiles, coarse_ids = inputs
        offset = position * bundle * extent
        stripe = lax.dynamic_slice_in_dim(transposed, offset, bundle * extent, 1).reshape(
            height, bundle, extent
        )
        product = jnp.einsum(
            "rfa,fkab->rfkb", stripe, bundle_tiles, preferred_element_type=jnp.float32
        )
        tiled = running.reshape(height, -1, extent)
        tiled = tiled.at[:, coarse_ids, :].add(product.reshape(height, bundle * per_block, extent))
        return (tiled.reshape(height, -1), None)

    counter = jnp.arange(blocks // bundle, dtype=jnp.int32)
    summed, _ = lax.scan(one_group, summed, (counter, tile_groups, column_groups))
    return summed


def body(p_tiles, p_cols, q_tiles, q_cols):
    extent = p_tiles.shape[2]
    tile_count = lax.axis_size("row")
    expanded = spread_tiles(p_tiles, p_cols, tile_count)
    transposed = lax.all_to_all(expanded, "row", split_axis=0, concat_axis=1, tiled=True)
    empty = jnp.zeros((transposed.shape[0], tile_count * extent), jnp.float32)
    partial_sum = fold_tiles(
        empty,
        transposed,
        lax.all_gather(q_tiles, "row", axis=0, tiled=True),
        lax.all_gather(q_cols, "row", axis=0, tiled=True),
    )
    return lax.psum_scatter(partial_sum, "col", scatter_dimension=1, tiled=True)


def solution(mesh):
    placed = (
        P(("row", "col"), None, None, None),
        P(("row", "col"), None),
        P(("row", "col"), None, None, None),
        P(("row", "col"), None),
    )
    return jax.shard_map(
        body, mesh=mesh, in_specs=placed, out_specs=P("row", "col"), check_vma=False
    )
```

profile of v0, /device:TPU:1, one launch (start us, length us, event | category | flops | bytes accessed | tf_op | source)
XLA Modules:
  0.0 604.4 jit_solution(11690526982969184347)
XLA Ops:
  9.3 3.0 broadcast_in_dim.18
  12.3 2.3 scatter_fusion.1
  14.5 6.5 %copy.24 = bf16[32,128,4,128]{1,3,2,0:T(8,128)(2,1)} copy(bf16[32,128,4,128]{3,1,2,0:T(8,128)(2,1)} %scatter_fusion.1) | data formatting | bytes 8388608 | tf_op jit(solution)/shard_map/scatter | solution.py:13
  21.0 12.8 %all-to-all-start = ((bf16[32,128,512]{1,2,0:T(8,128)(2,1)}), bf16[32,128,512]{1,2,0:T(8,128)(2,1)}, u32[]{:S(2)}, u32[]{:S(2)}) async-start(bf16[32,128,512]{1,2,0:T(8,128)(2,1)} %bitcast.65), calls=%async_computation | async-start | bytes 8388608 | tf_op jit(solution)/shard_map/all_to_all | solution.py:46
  33.8 154.7 %all-gather = s32[32,4,6]{2,1,0:T(4,128)S(1)} all-gather(s32[1,4,6]{2,1,0:T(4,128)S(1)} %bitcast.68), channel_id=1, replica_groups=mesh['row'=32,'col'=8] {'row'}, dimensions={0}, use_global_device_ids=true | all-gather | bytes 3168 | tf_op jit(solution)/shard_map/all_gather | solution.py:52
  188.6 77.6 %all-gather.3.cloned.1.call-done = bf16[128,6,128,128]{3,2,1,0:T(8,128)(2,1)} async-done(((bf16[4,6,128,128]{3,2,1,0:T(8,128)(2,1)}), bf16[128,6,128,128]{3,2,1,0:T(8,128)(2,1)}) %all-gather.3.cloned.1.call-update) | async-done | bytes 25165840 | tf_op jit(solution)/shard_map/all_gather | solution.py:51
  267.7 274.9 %while.12 = (s32[]{:T(128)}, f32[128,4096]{0,1:T(8,128)}, s32[16,48]{1,0:T(8,128)S(1)}, bf16[16,8,6,128,128]{4,3,2,1,0:T(8,128)(2,1)}, s32[16]{0:T(128)S(1)}, /*...) while((s32[]{:T(128)}, f32[128,4096]{0,1:T(8,128)}, ...), condition=%wide.region_3.4_spmd, body=%wide.region_1.3_spmd.sunk | while | flops 202113168 | bytes 29623528 | solution.py:38
  269.9 2.1 fusion.17
  272.0 2.4 copy.35
  276.3 6.7 %scatter_fusion = f32[128,32,128]{2,0,1:T(8,128)S(1)} fusion(f32[128,32,128]{2,0,1:T(8,128)S(1)} %copy.34, s32[48]{0:T(128)S(1)} %fusion.16, f32[48,128,128]{2,1,0:T(8,128)} %bitcast.61), kind=kCustom, calls=%fused_computation.clone.1 | custom fusion | flops 786432 | bytes 9437376 | tf_op jit(solution)/shard_map/while/body/eval_jaxpr/scatter-add | solution.py:34
  289.2 2.4 copy.35
  293.5 6.7 %scatter_fusion = f32[128,32,128]{2,0,1:T(8,128)S(1)} fusion(f32[128,32,128]{2,0,1:T(8,128)S(1)} %copy.34, s32[48]{0:T(128)S(1)} %fusion.16, f32[48,128,128]{2,1,0:T(8,128)} %bitcast.61), kind=kCustom, calls=%fused_computation.clone.1 | custom fusion | flops 786432 | bytes 9437376 | tf_op jit(solution)/shard_map/while/body/eval_jaxpr/scatter-add | solution.py:34
  304.3 2.1 fusion.17
  306.4 2.4 copy.35
  310.7 6.7 %scatter_fusion = f32[128,32,128]{2,0,1:T(8,128)S(1)} fusion(f32[128,32,128]{2,0,1:T(8,128)S(1)} %copy.34, s32[48]{0:T(128)S(1)} %fusion.16, f32[48,128,128]{2,1,0:T(8,128)} %bitcast.61), kind=kCustom, calls=%fused_computation.clone.1 | custom fusion | flops 786432 | bytes 9437376 | tf_op jit(solution)/shard_map/while/body/eval_jaxpr/scatter-add | solution.py:34
  323.5 2.4 copy.35
  327.8 6.7 %scatter_fusion = f32[128,32,128]{2,0,1:T(8,128)S(1)} fusion(f32[128,32,128]{2,0,1:T(8,128)S(1)} %copy.34, s32[48]{0:T(128)S(1)} %fusion.16, f32[48,128,128]{2,1,0:T(8,128)} %bitcast.61), kind=kCustom, calls=%fused_computation.clone.1 | custom fusion | flops 786432 | bytes 9437376 | tf_op jit(solution)/shard_map/while/body/eval_jaxpr/scatter-add | solution.py:34
  340.7 2.4 copy.35
  345.0 6.7 %scatter_fusion = f32[128,32,128]{2,0,1:T(8,128)S(1)} fusion(f32[128,32,128]{2,0,1:T(8,128)S(1)} %copy.34, s32[48]{0:T(128)S(1)} %fusion.16, f32[48,128,128]{2,1,0:T(8,128)} %bitcast.61), kind=kCustom, calls=%fused_computation.clone.1 | custom fusion | flops 786432 | bytes 9437376 | tf_op jit(solution)/shard_map/while/body/eval_jaxpr/scatter-add | solution.py:34
  357.9 2.4 copy.35
  362.2 6.7 %scatter_fusion = f32[128,32,128]{2,0,1:T(8,128)S(1)} fusion(f32[128,32,128]{2,0,1:T(8,128)S(1)} %copy.34, s32[48]{0:T(128)S(1)} %fusion.16, f32[48,128,128]{2,1,0:T(8,128)} %bitcast.61), kind=kCustom, calls=%fused_computation.clone.1 | custom fusion | flops 786432 | bytes 9437376 | tf_op jit(solution)/shard_map/while/body/eval_jaxpr/scatter-add | solution.py:34
  373.0 2.1 fusion.17
  375.1 2.4 copy.35
  379.4 6.7 %scatter_fusion = f32[128,32,128]{2,0,1:T(8,128)S(1)} fusion(f32[128,32,128]{2,0,1:T(8,128)S(1)} %copy.34, s32[48]{0:T(128)S(1)} %fusion.16, f32[48,128,128]{2,1,0:T(8,128)} %bitcast.61), kind=kCustom, calls=%fused_computation.clone.1 | custom fusion | flops 786432 | bytes 9437376 | tf_op jit(solution)/shard_map/while/body/eval_jaxpr/scatter-add | solution.py:34
  392.3 2.4 copy.35
  396.6 6.7 %scatter_fusion = f32[128,32,128]{2,0,1:T(8,128)S(1)} fusion(f32[128,32,128]{2,0,1:T(8,128)S(1)} %copy.34, s32[48]{0:T(128)S(1)} %fusion.16, f32[48,128,128]{2,1,0:T(8,128)} %bitcast.61), kind=kCustom, calls=%fused_computation.clone.1 | custom fusion | flops 786432 | bytes 9437376 | tf_op jit(solution)/shard_map/while/body/eval_jaxpr/scatter-add | solution.py:34
  409.4 2.4 copy.35
  413.7 6.7 %scatter_fusion = f32[128,32,128]{2,0,1:T(8,128)S(1)} fusion(f32[128,32,128]{2,0,1:T(8,128)S(1)} %copy.34, s32[48]{0:T(128)S(1)} %fusion.16, f32[48,128,128]{2,1,0:T(8,128)} %bitcast.61), kind=kCustom, calls=%fused_computation.clone.1 | custom fusion | flops 786432 | bytes 9437376 | tf_op jit(solution)/shard_map/while/body/eval_jaxpr/scatter-add | solution.py:34
  424.6 2.1 fusion.17
  426.6 2.4 copy.35
  430.9 6.7 %scatter_fusion = f32[128,32,128]{2,0,1:T(8,128)S(1)} fusion(f32[128,32,128]{2,0,1:T(8,128)S(1)} %copy.34, s32[48]{0:T(128)S(1)} %fusion.16, f32[48,128,128]{2,1,0:T(8,128)} %bitcast.61), kind=kCustom, calls=%fused_computation.clone.1 | custom fusion | flops 786432 | bytes 9437376 | tf_op jit(solution)/shard_map/while/body/eval_jaxpr/scatter-add | solution.py:34
  443.8 2.4 copy.35
  448.1 6.7 %scatter_fusion = f32[128,32,128]{2,0,1:T(8,128)S(1)} fusion(f32[128,32,128]{2,0,1:T(8,128)S(1)} %copy.34, s32[48]{0:T(128)S(1)} %fusion.16, f32[48,128,128]{2,1,0:T(8,128)} %bitcast.61), kind=kCustom, calls=%fused_computation.clone.1 | custom fusion | flops 786432 | bytes 9437376 | tf_op jit(solution)/shard_map/while/body/eval_jaxpr/scatter-add | solution.py:34
  461.0 2.4 copy.35
  465.3 6.7 %scatter_fusion = f32[128,32,128]{2,0,1:T(8,128)S(1)} fusion(f32[128,32,128]{2,0,1:T(8,128)S(1)} %copy.34, s32[48]{0:T(128)S(1)} %fusion.16, f32[48,128,128]{2,1,0:T(8,128)} %bitcast.61), kind=kCustom, calls=%fused_computation.clone.1 | custom fusion | flops 786432 | bytes 9437376 | tf_op jit(solution)/shard_map/while/body/eval_jaxpr/scatter-add | solution.py:34
  476.1 2.1 fusion.17
  478.2 2.4 copy.35
  482.5 6.7 %scatter_fusion = f32[128,32,128]{2,0,1:T(8,128)S(1)} fusion(f32[128,32,128]{2,0,1:T(8,128)S(1)} %copy.34, s32[48]{0:T(128)S(1)} %fusion.16, f32[48,128,128]{2,1,0:T(8,128)} %bitcast.61), kind=kCustom, calls=%fused_computation.clone.1 | custom fusion | flops 786432 | bytes 9437376 | tf_op jit(solution)/shard_map/while/body/eval_jaxpr/scatter-add | solution.py:34
  493.3 2.1 fusion.17
  495.3 2.4 copy.35
  499.6 6.7 %scatter_fusion = f32[128,32,128]{2,0,1:T(8,128)S(1)} fusion(f32[128,32,128]{2,0,1:T(8,128)S(1)} %copy.34, s32[48]{0:T(128)S(1)} %fusion.16, f32[48,128,128]{2,1,0:T(8,128)} %bitcast.61), kind=kCustom, calls=%fused_computation.clone.1 | custom fusion | flops 786432 | bytes 9437376 | tf_op jit(solution)/shard_map/while/body/eval_jaxpr/scatter-add | solution.py:34
  510.5 2.1 fusion.17
  512.5 2.4 copy.35
  516.8 6.7 %scatter_fusion = f32[128,32,128]{2,0,1:T(8,128)S(1)} fusion(f32[128,32,128]{2,0,1:T(8,128)S(1)} %copy.34, s32[48]{0:T(128)S(1)} %fusion.16, f32[48,128,128]{2,1,0:T(8,128)} %bitcast.61), kind=kCustom, calls=%fused_computation.clone.1 | custom fusion | flops 786432 | bytes 9437376 | tf_op jit(solution)/shard_map/while/body/eval_jaxpr/scatter-add | solution.py:34
  529.7 2.4 copy.35
  534.0 6.7 %scatter_fusion = f32[128,32,128]{2,0,1:T(8,128)S(1)} fusion(f32[128,32,128]{2,0,1:T(8,128)S(1)} %copy.34, s32[48]{0:T(128)S(1)} %fusion.16, f32[48,128,128]{2,1,0:T(8,128)} %bitcast.61), kind=kCustom, calls=%fused_computation.clone.1 | custom fusion | flops 786432 | bytes 9437376 | tf_op jit(solution)/shard_map/while/body/eval_jaxpr/scatter-add | solution.py:34
  542.6 2.9 copy.26
  545.5 52.1 %reduce-scatter.2.cloned.1.call-done = f32[128,512]{1,0:T(8,128)} async-done(((f32[128,4096]{1,0:T(8,128)}), f32[128,512]{1,0:T(8,128)}) %reduce-scatter.2.cloned.1.call-update) | async-done | bytes 262160 | tf_op jit(solution)/shard_map/reduce_scatter | solution.py:54
  (103 shorter events, 108.7 us)
Async XLA Ops:
  6.5 259.7 %all-gather.3.cloned.1.call-start = ((), (), s32[]{:S(2)}) async-start(), calls=%async_computation.2 | async-start | bytes 25952256 | tf_op jit(solution)/shard_map/all_gather | solution.py:51
  21.0 12.8 %copy-start = (s32[4,6]{1,0:T(4,128)S(1)}, s32[4,6]{1,0:T(4,128)}, u32[]{:S(2)}) copy-start(s32[4,6]{1,0:T(4,128)} %param.9) | copy-start | bytes 292
  21.0 167.6 %all-to-all-start = ((bf16[32,128,512]{1,2,0:T(8,128)(2,1)}), bf16[32,128,512]{1,2,0:T(8,128)(2,1)}, u32[]{:S(2)}, u32[]{:S(2)}) async-start(bf16[32,128,512]{1,2,0:T(8,128)(2,1)} %bitcast.65), calls=%async_computation | async-start | bytes 8388608 | tf_op jit(solution)/shard_map/all_to_all | solution.py:46
  33.8 563.8 %reduce-scatter.2.cloned.1.call-start = ((), (), s32[]{:S(2)}) async-start(), calls=%async_computation.3 | async-start | bytes 2359296 | tf_op jit(solution)/shard_map/reduce_scatter | solution.py:54
Sparse Core Ops, SparseCore 0:
  10.1 256.0 all-gather.2
  545.6 51.9 reduce-scatter.1
where the time goes:
time: 608 us; the launch traced here: 604 us
  blocking collectives  155 us (25%)
  local copies, waits for them, and re-layouts  141 us (23%)
  waiting for transfers between devices  130 us (21%)
  other arithmetic  109 us (18%)
  matrix products  33 us (5%)
  between operations  13.4 us (2%)
  starting transfers between devices  12.8 us (2%)
  loops' own time  10.5 us (2%)
    all_gather x1, blocking collectives, body(): lax.all_gather(q_cols, 'row', axis=0, tiled=True)  155 us
    scatter-add x16, other arithmetic, one_group(): tiled.at[:, coarse_ids, :]  108 us
    all_gather x1, waiting for transfers between devices, body(): lax.all_gather(q_tiles, 'row', axis=0, tiled=True)  77.6 us
    reduce_scatter x1, waiting for transfers between devices, body(): return lax.psum_scatter(partial_sum, 'col', scatter_dimension=1, tiled=True)  52.1 us
    reshape x16, local copies, waits for them, and re-layouts, one_group(): product.reshape(height, bundle * per_block, extent)  37.8 us
    dot_general x16, matrix products, one_group(): jnp.einsum('rfa,fkab->rfkb', stripe, bundle_tiles, preferred_element_type...  33 us
    reshape x16, local copies, waits for them, and re-layouts, one_group(): tiled = running.reshape(height, -1, extent)  30.7 us
    scatter-add x16, local copies, waits for them, and re-layouts, one_group(): tiled.at[:, coarse_ids, :]  29.2 us
  transfers between devices with their start and end apart: 3, of which 2 were waited for; matrix products, arithmetic and copies ran while one was open for 2% of the time, Pallas kernels for 0%

commit v1 on v0

--- a/solution.py
+++ b/solution.py
@@ -48,7 +48,9 @@
     partial_sum = fold_tiles(
         empty,
         transposed,
-        lax.all_gather(q_tiles, "row", axis=0, tiled=True),
+        jnp.concatenate(
+            lax.all_to_all(jnp.stack([q_tiles] * lax.axis_size("row")), "row", 0, 0), axis=0
+        ),
         lax.all_gather(q_cols, "row", axis=0, tiled=True),
     )
     return lax.psum_scatter(partial_sum, "col", scatter_dimension=1, tiled=True)

time: 608 us -> 1080 us (1.78)
  blocking collectives: 155 us -> 593 us
  waiting for transfers between devices: 130 us -> 144 us
  local copies, waits for them, and re-layouts: 141 us -> 153 us
    all_gather x1, blocking collectives: 155 us -> 593 us  [body(): lax.all_gather(q_cols, 'row', axis=0, tiled=True)]
    all_to_all x1, waiting for transfers between devices: 0.01 us -> 95.8 us  [body(): lax.all_to_all(expanded, 'row', split_axis=0, concat_axis=1, tiled=True)]
    all_gather x1 -> x0, waiting for transfers between devices: 77.6 us -> none  [body(): lax.all_gather(q_tiles, 'row', axis=0, tiled=True)]
  transfers between devices with their start and end apart: 3 -> 3, of which waited for: 2 -> 2; matrix products, arithmetic and copies ran while one was open for 2% -> 0% of each run, Pallas kernels for 0% -> 0%
where the time goes in v1:
time: 1080 us; the launch traced here: 1070 us
  blocking collectives  593 us (55%)
  local copies, waits for them, and re-layouts  153 us (14%)
  waiting for transfers between devices  144 us (13%)
  other arithmetic  109 us (10%)
  matrix products  31.6 us (3%)
  starting transfers between devices  20.2 us (2%)
  between operations  13.5 us (1%)
    all_gather x1, blocking collectives, body(): lax.all_gather(q_cols, 'row', axis=0, tiled=True)  593 us
    scatter-add x16, other arithmetic, one_group(): tiled.at[:, coarse_ids, :]  108 us
    all_to_all x1, waiting for transfers between devices, body(): lax.all_to_all(expanded, 'row', split_axis=0, concat_axis=1, tiled=True)  95.8 us
    reduce_scatter x1, waiting for transfers between devices, body(): return lax.psum_scatter(partial_sum, 'col', scatter_dimension=1, tiled=True)  48.6 us
    reshape x16, local copies, waits for them, and re-layouts, one_group(): product.reshape(height, bundle * per_block, extent)  39.3 us
    dot_general x16, matrix products, one_group(): jnp.einsum('rfa,fkab->rfkb', stripe, bundle_tiles, preferred_element_type...  31.6 us
    reshape x16, local copies, waits for them, and re-layouts, one_group(): tiled = running.reshape(height, -1, extent)  30.7 us
    scatter-add x16, local copies, waits for them, and re-layouts, one_group(): tiled.at[:, coarse_ids, :]  30.7 us
  transfers between devices with their start and end apart: 3, of which 2 were waited for; matrix products, arithmetic and copies ran while one was open for 0% of the time, Pallas kernels for 0%

profile of v1, /device:TPU:1, one launch (start us, length us, event | category | flops | bytes accessed | tf_op | source)
XLA Modules:
  0.0 1073.2 jit_solution(12527763792433293843)
XLA Ops:
  8.5 3.0 broadcast_in_dim.18
  11.6 2.3 scatter_fusion.1
  13.9 6.5 copy.25
  20.3 12.7 %all-to-all-start.1 = ((bf16[32,128,512]{1,2,0:T(8,128)(2,1)}), bf16[32,128,512]{1,2,0:T(8,128)(2,1)}, u32[]{:S(2)}, u32[]{:S(2)}) async-start(bf16[32,128,512]{1,2,0:T(8,128)(2,1)} %bitcast.64), calls=%async_computation.1 | async-start | bytes 8388608 | tf_op jit(solution)/shard_map/all_to_all | solution.py:46
  33.5 95.8 %all-to-all-done.1 = bf16[32,128,512]{1,2,0:T(8,128)(2,1)} async-done(((bf16[32,128,512]{1,2,0:T(8,128)(2,1)}), bf16[32,128,512]{1,2,0:T(8,128)(2,1)}, u32[]{:S(2)}, u32[]{:S(2)}) %all-to-all-start.1) | async-done | bytes 4194336 | tf_op jit(solution)/shard_map/all_to_all | solution.py:46
  129.2 9.2 stack.2
  138.4 7.4 all-to-all-start
  145.9 592.5 %all-gather = s32[32,4,6]{2,1,0:T(4,128)S(1)} all-gather(s32[1,4,6]{2,1,0:T(4,128)S(1)} %bitcast.66), channel_id=1, replica_groups=mesh['row'=32,'col'=8] {'row'}, dimensions={0}, use_global_device_ids=true | all-gather | bytes 3168 | tf_op jit(solution)/shard_map/all_gather | solution.py:54
  740.1 274.8 %while.12 = (s32[]{:T(128)}, f32[128,4096]{0,1:T(8,128)}, s32[16,48]{1,0:T(8,128)S(1)}, bf16[16,8,6,128,128]{3,4,2,1,0:T(8,128)(2,1)}, s32[16]{0:T(128)S(1)}, /*...) while((s32[]{:T(128)}, f32[128,4096]{0,1:T(8,128)}, ...), condition=%wide.region_3.4_spmd, body=%wide.region_1.3_spmd.sunk | while | flops 202113168 | bytes 29623528 | solution.py:38
  742.2 2.0 fusion.17
  744.2 2.5 copy.34
  748.6 6.7 scatter_fusion
  759.4 2.0 fusion.17
  761.4 2.5 copy.34
  765.8 6.7 scatter_fusion
  778.6 2.5 copy.34
  783.0 6.7 scatter_fusion
  795.7 2.5 copy.34
  800.1 6.7 scatter_fusion
  812.9 2.5 copy.34
  817.3 6.7 scatter_fusion
  830.1 2.5 copy.34
  834.5 6.7 scatter_fusion
  847.3 2.5 copy.34
  851.7 6.7 scatter_fusion
  862.5 2.0 fusion.17
  864.4 2.5 copy.34
  868.8 6.7 scatter_fusion
  881.6 2.5 copy.34
  886.0 6.7 scatter_fusion
  898.8 2.5 copy.34
  903.2 6.7 scatter_fusion
  916.0 2.5 copy.34
  920.4 6.7 scatter_fusion
  933.1 2.5 copy.34
  937.5 6.7 scatter_fusion
  948.3 2.0 fusion.17
  950.3 2.5 copy.34
  954.7 6.7 scatter_fusion
  967.5 2.5 copy.34
  971.9 6.7 scatter_fusion
  982.7 2.0 fusion.17
  984.7 2.5 copy.34
  989.1 6.7 scatter_fusion
  1001.8 2.5 copy.34
  1006.2 6.7 scatter_fusion
  1014.9 2.9 copy.26
  1017.8 48.6 %reduce-scatter.2.cloned.1.call-done = f32[128,512]{1,0:T(8,128)} async-done(((f32[128,4096]{1,0:T(8,128)}), f32[128,512]{1,0:T(8,128)}) %reduce-scatter.2.cloned.1.call-update) | async-done | bytes 262160 | tf_op jit(solution)/shard_map/reduce_scatter | solution.py:56
  (106 shorter events, 112.2 us)
Async XLA Ops:
  20.3 12.7 %copy-start = (bf16[4,6,128,128]{3,2,1,0:T(8,128)(2,1)S(1)}, bf16[4,6,128,128]{3,2,1,0:T(8,128)(2,1)}, u32[]{:S(2)}) copy-start(bf16[4,6,128,128]{3,2,1,0:T(8,128)(2,1)} %param.8) | copy-start | bytes 2359300
  20.3 108.9 %all-to-all-start.1 = ((bf16[32,128,512]{1,2,0:T(8,128)(2,1)}), bf16[32,128,512]{1,2,0:T(8,128)(2,1)}, u32[]{:S(2)}, u32[]{:S(2)}) async-start(bf16[32,128,512]{1,2,0:T(8,128)(2,1)} %bitcast.64), calls=%async_computation.1 | async-start | bytes 8388608 | tf_op jit(solution)/shard_map/all_to_all | solution.py:46
  138.4 7.5 copy-start.1
  138.4 600.1 %all-to-all-start = ((bf16[32,4,6,128,128]{3,4,2,1,0:T(8,128)(2,1)}), bf16[32,4,6,128,128]{3,4,2,1,0:T(8,128)(2,1)}, u32[]{:S(2)}, u32[]{:S(2)}) async-start(bf16[32,4,6,128,128]{3,4,2,1,0:T(8,128)(2,1)} %stack.2), calls=%async_computation | async-start | bytes 50331648 | tf_op jit(solution)/shard_map/all_to_all | solution.py:52
  145.8 920.6 %reduce-scatter.2.cloned.1.call-start = ((), (), s32[]{:S(2)}) async-start(), calls=%async_computation.3 | async-start | bytes 2359296 | tf_op jit(solution)/shard_map/reduce_scatter | solution.py:56
Sparse Core Ops, SparseCore 0:
  1018.0 48.3 reduce-scatter.1
